TPU v7x, 32 devices: a whole 2x2x4 slice. The times are simulated.
32 devices in a mesh: az: 4 (over z), rad: 2 (over x), ax: 4 (over y, core).
Axes of the slice: x: 2, y: 2, z: 4, core: 2. Of those that a mesh axis runs over, the one named last changes fastest.
Arguments:
- cycle: float32 [4, 5, 512, 4096], P(None, None, ('rad', 'ax'), 'az'), may hold values from -6 to 6
- field: float32 [5, 64, 8, 4096], P(None, 'rad', 'ax', 'az'), may hold values from -6 to 6
- shift: int32 [1], replicated, may hold values from 0 to 4095
- owner: int32 [64, 8], P('rad', 'ax'), may hold values 0 or 1
Outputs:
- field_next: float32 [5, 64, 8, 4096], P(None, 'rad', 'ax', 'az')
- shifted_cycle: float32 [4, 5, 512, 4096], P(None, None, ('rad', 'ax'), 'az')
All inputs are finite; a program needn't handle non-finite values. No bound on the sum of `owner` on one device may be relied on, other than what follows from the above.
Results may differ from a plain program's by a relative error of at most 0.00007.
Values sent between devices are 32-bit elements; how exact they have to be, the bound alone decides.
A program may use at most 192 MiB of HBM per device.

v0:
```python
import math
import jax
import jax.numpy as jnp
from jax import lax
from jax.sharding import PartitionSpec as P

KR = 8
LAYER_WEIGHTS = (0.4, 0.3, 0.2, 0.1)
AXIAL_SPEEDS = (0.35, 0.2, 0.3, 0.25, 0.4)
DIFFUSION = 0.15
SWIRL_SPEED = 0.1


def padded(array, sides, width):
    for axis, dim in sides:
        devices, length = (lax.axis_size(axis), array.shape[dim])
        up = [(i, (i + 1) % devices) for i in range(devices - 1)]
        down = [(j, i) for i, j in up]
        last = lax.slice_in_dim(array, length - width, length, axis=dim)
        leading = lax.slice_in_dim(array, 0, width, axis=dim)
        before = lax.ppermute(last, axis, up)
        after = lax.ppermute(leading, axis, down)
        array = jnp.concatenate([before, array, after], axis=dim)
    return array


def turn_table(first, second, modulus):
    product = jnp.remainder(first[:, None] * second[None, :], modulus).astype(jnp.float32)
    angle = product * (2.0 * math.pi / modulus)
    return (jnp.cos(angle), jnp.sin(angle))


def spectral_shift(rows, shift_value):
    count, length = rows.shape
    half_bits = (length.bit_length() - 1) // 2
    outer = 2**half_bits
    inner = length // outer
    hp = lax.Precision.HIGHEST
    outer_index = jnp.arange(outer, dtype=jnp.int32)
    inner_index = jnp.arange(inner, dtype=jnp.int32)
    cos_outer, sin_outer = turn_table(outer_index, outer_index, outer)
    cos_inner, sin_inner = turn_table(inner_index, inner_index, inner)
    cos_twist, sin_twist = turn_table(outer_index, inner_index, length)
    grid = rows.reshape(count, outer, inner)
    section_re = jnp.einsum("bpq,pk->bkq", grid, cos_outer, precision=hp)
    section_im = -jnp.einsum("bpq,pk->bkq", grid, sin_outer, precision=hp)
    twist_re = section_re * cos_twist + section_im * sin_twist
    twist_im = section_im * cos_twist - section_re * sin_twist
    spec_re = jnp.einsum("bkq,qm->bkm", twist_re, cos_inner, precision=hp) + jnp.einsum(
        "bkq,qm->bkm", twist_im, sin_inner, precision=hp
    )
    spec_im = jnp.einsum("bkq,qm->bkm", twist_im, cos_inner, precision=hp) - jnp.einsum(
        "bkq,qm->bkm", twist_re, sin_inner, precision=hp
    )
    wave = outer_index[:, None] + outer * inner_index[None, :]
    folded = jnp.minimum(wave, length - wave)
    filt = (3 * folded < length).astype(jnp.float32)
    phase = jnp.remainder(wave * shift_value, length).astype(jnp.float32) * (2.0 * math.pi / length)
    gain_re = filt * jnp.cos(phase)
    gain_im = -filt * jnp.sin(phase)
    mixed_re = spec_re * gain_re - spec_im * gain_im
    mixed_im = spec_re * gain_im + spec_im * gain_re
    back_re = jnp.einsum("bkm,qm->bkq", mixed_re, cos_inner, precision=hp) - jnp.einsum(
        "bkm,qm->bkq", mixed_im, sin_inner, precision=hp
    )
    back_im = jnp.einsum("bkm,qm->bkq", mixed_im, cos_inner, precision=hp) + jnp.einsum(
        "bkm,qm->bkq", mixed_re, sin_inner, precision=hp
    )
    turn_re = back_re * cos_twist - back_im * sin_twist
    turn_im = back_im * cos_twist + back_re * sin_twist
    result = jnp.einsum("bkq,pk->bpq", turn_re, cos_outer, precision=hp) - jnp.einsum(
        "bkq,pk->bpq", turn_im, sin_outer, precision=hp
    )
    return (result / length).reshape(count, length)


def on_device(cycle, field, shift, owner):
    layers, variables, radial, sector = cycle.shape
    stacked = cycle.reshape(layers * variables, radial, sector)
    shift_value = shift[0]
    piece = lax.all_to_all(stacked, "az", split_axis=1, concat_axis=2, tiled=True)
    moved = spectral_shift(piece.reshape(-1, piece.shape[2]), shift_value).reshape(piece.shape)
    shifted_flat = lax.all_to_all(moved, "az", split_axis=2, concat_axis=1, tiled=True)
    shifted_cycle = shifted_flat.reshape(layers, variables, radial, sector)
    weights = jnp.array(LAYER_WEIGHTS, jnp.float32)
    depth, count, rows, width = shifted_cycle.shape
    grouped = shifted_cycle.reshape(depth, count, rows // KR, KR, width)
    ghost = lax.all_gather(
        jnp.einsum("l,lvrkt->vrt", weights, grouped, precision=lax.Precision.HIGHEST) / KR,
        "ax",
        axis=1,
        tiled=True,
    )
    mask = owner.astype(jnp.float32)[None, :, :, None]
    speeds = jnp.array(AXIAL_SPEEDS, jnp.float32)[:, None, None, None]
    at_inlet = lax.axis_index("ax") == 0

    def rates(state):
        radial_pad = padded(state, (("rad", 1),), 1)
        axial_pad = padded(state, (("ax", 2),), 1)
        lower = jnp.where(at_inlet, ghost, axial_pad[:, :, 0])
        outward = radial_pad[:, 2:]
        inward = radial_pad[:, :-2]
        above = axial_pad[:, :, 2:]
        below = jnp.concatenate([lower[:, :, None], axial_pad[:, :, 1:-2]], axis=2)
        return mask * (
            DIFFUSION * (outward + inward + above + below - 4.0 * state)
            - 0.5 * speeds * (above - below)
            - 0.5 * SWIRL_SPEED * (outward - inward)
        )

    first = rates(field)
    second = rates(field + 0.5 * first)
    third = rates(field + 0.5 * second)
    fourth = rates(field + third)
    field_next = field + (first + 2.0 * second + 2.0 * third + fourth) / 6.0
    return (field_next, shifted_cycle)


def solution(mesh):
    in_specs = (P(None, None, ("rad", "ax"), "az"), P(None, "rad", "ax", "az"), P(), P("rad", "ax"))
    out_specs = (P(None, "rad", "ax", "az"), P(None, None, ("rad", "ax"), "az"))
    return jax.shard_map(
        on_device, mesh=mesh, in_specs=in_specs, out_specs=out_specs, check_vma=False
    )
```

profile of v0, /device:TPU:1, one launch (start us, length us, event | category | flops | bytes accessed | tf_op | source)
XLA Modules:
  0.0 716.4 jit_solution(15796967327889109579)
XLA Ops:
  0.6 8.2 %copy.187 = f32[20,64,1024]{2,0,1:T(8,128)} copy(f32[20,64,1024]{2,1,0:T(8,128)} %bitcast.97) | data formatting | bytes 10485760 | tf_op jit(solution)/shard_map/reshape | solution.py:79
  8.8 5.6 all-to-all-start
  15.6 137.3 %all-to-all-done = f32[20,64,1024]{2,0,1:T(8,128)} async-done(((f32[20,64,1024]{2,0,1:T(8,128)}), f32[20,64,1024]{2,0,1:T(8,128)}, u32[]{:S(2)}, u32[]{:S(2)}) %all-to-all-start) | async-done | bytes 5242912 | tf_op jit(solution)/shard_map/all_to_all | solution.py:81
  152.9 8.5 %copy.189 = f32[20,16,4,1024]{3,2,1,0:T(4,128)} copy(f32[20,16,4,1024]{3,0,1,2:T(8,128)} %bitcast.5) | data formatting | bytes 10485760 | tf_op jit(solution)/shard_map/all_to_all | solution.py:81
  161.4 9.6 %reshape_reshape.9 = f32[320,64,64]{2,1,0:T(8,128)} reshape(f32[20,16,4,1024]{3,2,1,0:T(4,128)} %copy.189) | data formatting | bytes 10485760 | tf_op jit(solution)/shard_map/reshape;reshape | solution.py:44
  171.1 11.8 %copy.191 = f32[320,64,64]{0,1,2:T(8,128)} copy(f32[320,64,64]{2,1,0:T(8,128)} %reshape_reshape.9) | data formatting | bytes 10485760 | tf_op jit(solution)/shard_map/reshape;reshape | solution.py:44
  182.9 8.7 %fusion.44 = f32[64,320,64]{1,0,2:T(8,128)S(1)} fusion(f32[320,64,64]{0,1,2:T(8,128)} %copy.191), kind=kOutput, calls=%fused_computation.85 | convolution fusion | flops 1006690304 | bytes 10485760 | tf_op jit(solution)/shard_map/bpq,pk->bkq/dot_general | solution.py:46
  191.6 7.6 %add_bitcast_fusion = (f32[320,64,64]{0,1,2:T(8,128)S(1)}, f32[320,64,64]{0,1,2:T(8,128)S(1)}) fusion(f32[64,320,64]{1,0,2:T(8,128)S(1)} %fusion.44, f32[64,64]{0,1:T(8,128)S(1)} %copy.195, f32[64,64]{0,1:T(8,128)S(1)} %copy.192, f32[320,64,64]{0,1,2:T(8,128)S(1)} %copy-done.2), kind=kOutput, calls=%fused_computation.10 | convolution fusion | flops 1015865344 | bytes 21004288 | tf_op jit(solution)/shard_map/bpq,pk->bkq/dot_general | solution.py:45
  199.2 14.0 %fusion.10 = f32[320,64,64]{0,2,1:T(8,128)} fusion(f32[320,64,64]{0,1,2:T(8,128)S(1)} %get-tuple-element.16), kind=kOutput, calls=%fused_computation.17 | convolution fusion | flops 1006690304 | bytes 10485760 | tf_op jit(solution)/shard_map/bkq,qm->bkm/dot_general | solution.py:49
  213.2 13.2 %fusion.8 = f32[320,64,64]{0,2,1:T(8,128)} fusion(f32[320,64,64]{0,1,2:T(8,128)S(1)} %get-tuple-element.16), kind=kOutput, calls=%fused_computation.15 | convolution fusion | flops 1006690304 | bytes 10485760 | tf_op jit(solution)/shard_map/bkq,qm->bkm/dot_general | solution.py:52
  226.4 13.3 %fusion.6 = f32[320,64,64]{0,2,1:T(8,128)} fusion(f32[320,64,64]{0,1,2:T(8,128)S(1)} %get-tuple-element.17), kind=kOutput, calls=%fused_computation.13 | convolution fusion | flops 1006690304 | bytes 10485760 | tf_op jit(solution)/shard_map/bkq,qm->bkm/dot_general | solution.py:49
  239.7 19.1 %multiply_subtract_fusion.1 = (f32[320,64,64]{0,2,1:T(8,128)}, f32[320,64,64]{0,2,1:T(8,128)S(1)}) fusion(f32[64,64]{1,0:T(8,128)S(1)} %get-tuple-element.35, f32[64,64]{1,0:T(8,128)S(1)} %get-tuple-element.34, f32[320,64,64]{0,2,1:T(8,128)} %fusion.8, f32[320,64,64]{0,2,1:T(8,128)} %fusion.10, f32[320,64,64]{0,2,1:T(8,128)} %fusion.6, ...), kind=kOutput, calls=%fused_computation.8 | convolution fusion | flops 1017176064 | bytes 31490048 | tf_op jit(solution)/shard_map/bkq,qm->bkm/dot_general | solution.py:52
  258.9 10.3 %fusion.38 = f32[320,64,64]{0,2,1:T(8,128)} fusion(f32[320,64,64]{0,2,1:T(8,128)} %get-tuple-element.14), kind=kOutput, calls=%fused_computation.79 | convolution fusion | flops 1006690304 | bytes 10485760 | tf_op jit(solution)/shard_map/bkm,qm->bkq/dot_general | solution.py:66
  269.2 7.8 %fusion.53 = f32[320,64,64]{0,2,1:T(8,128)} fusion(f32[320,64,64]{0,2,1:T(8,128)S(1)} %copy-done), kind=kOutput, calls=%fused_computation.94 | convolution fusion | flops 1006690304 | bytes 10485760 | tf_op jit(solution)/shard_map/bkm,qm->bkq/dot_general | solution.py:63
  277.0 7.9 %fusion.40 = f32[320,64,64]{0,2,1:T(8,128)} fusion(f32[320,64,64]{0,2,1:T(8,128)S(1)} %get-tuple-element.15), kind=kOutput, calls=%fused_computation.81 | convolution fusion | flops 1006690304 | bytes 10485760 | tf_op jit(solution)/shard_map/bkm,qm->bkq/dot_general | solution.py:63
  284.9 15.2 %multiply_subtract_fusion = (f32[320,64,64]{0,2,1:T(8,128)}, f32[320,64,64]{0,2,1:T(8,128)}) fusion(f32[64,64]{1,0:T(8,128)S(1)} %get-tuple-element.36, f32[64,64]{1,0:T(8,128)S(1)} %get-tuple-element.37, f32[320,64,64]{0,2,1:T(8,128)} %fusion.38, f32[320,64,64]{0,2,1:T(8,128)} %fusion.53, f32[320,64,64]{0,2,1:T(8,128)} %fusion.40, ...), kind=kOutput, calls=%fused_computation.6 | convolution fusion | flops 1017176064 | bytes 31490048 | tf_op jit(solution)/shard_map/bkm,qm->bkq/dot_general | solution.py:66
  300.1 12.4 %fusion = f32[64,320,64]{1,0,2:T(8,128)S(1)} fusion(f32[320,64,64]{0,2,1:T(8,128)} %get-tuple-element.13), kind=kOutput, calls=%fused_computation | convolution fusion | flops 1006690304 | bytes 10485760 | tf_op jit(solution)/shard_map/bkq,pk->bpq/dot_general | solution.py:71
  312.5 11.2 %multiply_bitcast_fusion = f32[320,64,64]{0,1,2:T(8,128)} fusion(f32[64,320,64]{1,0,2:T(8,128)S(1)} %fusion, f32[320,64,64]{0,2,1:T(8,128)S(1)} %copy-done.3), kind=kOutput, calls=%fused_computation.4 | convolution fusion | flops 1009311744 | bytes 15728640 | tf_op jit(solution)/shard_map/bkq,pk->bpq/dot_general | solution.py:71
  323.7 12.6 %copy.206 = f32[320,64,64]{2,1,0:T(8,128)} copy(f32[320,64,64]{0,1,2:T(8,128)} %multiply_bitcast_fusion) | data formatting | bytes 10485760 | tf_op jit(solution)/shard_map/div | solution.py:74
  336.2 9.7 %reshape_reshape.10 = f32[20,16,4096]{2,1,0:T(8,128)} reshape(f32[320,64,64]{2,1,0:T(8,128)} %copy.206) | data formatting | bytes 10485760 | tf_op jit(solution)/shard_map/reshape;reshape | solution.py:82
  346.0 18.7 %copy.207 = f32[20,16,4096]{0,1,2:T(8,128)} copy(f32[20,16,4096]{2,1,0:T(8,128)} %reshape_reshape.10) | data formatting | bytes 10485760 | tf_op jit(solution)/shard_map/reshape;reshape | solution.py:82
  364.7 56.1 %reshape.131 = f32[4,1,327680]{2,1,0:T(1,128)} reshape(f32[4096,16,20]{2,1,0:T(8,128)} %bitcast.92) | data formatting | bytes 10485760
  420.9 5.2 all-to-all-start.1
  427.5 4.3 collective-permute-start.3
  439.1 102.1 %all-to-all-done.1 = f32[4,1,327680]{2,1,0:T(1,128)} async-done(((f32[4,1,327680]{2,1,0:T(1,128)}), f32[4,1,327680]{2,1,0:T(1,128)}, u32[]{:S(2)}, u32[]{:S(2)}) %all-to-all-start.1) | async-done | bytes 5242912 | tf_op jit(solution)/shard_map/all_to_all | solution.py:83
  541.8 18.3 %reduce = f32[4,327680]{1,0:T(4,128)} reduce(f32[4,1,327680]{2,1,0:T(1,128)} %all-to-all-done.1, f32[]{:T(128)} %broadcast.363), dimensions={1}, to_apply=%all_to_all.25.reduce_sub_computation | reduce | bytes 10485764 | tf_op jit(solution)/shard_map/all_to_all | solution.py:83
  560.1 52.9 %reshape.132 = f32[4096,16,20]{2,1,0:T(8,128)} reshape(f32[4,327680]{1,0:T(4,128)} %reduce) | data formatting | bytes 10485760
  613.0 22.4 %copy.234 = f32[20,16,4,1024]{3,2,1,0:T(4,128)} copy(f32[20,16,4,1024]{0,1,3,2:T(8,128)} %bitcast.93) | data formatting | bytes 10485760 | tf_op jit(solution)/shard_map/all_to_all | solution.py:83
  635.4 9.2 %copy.209 = f32[20,4,16,1024]{3,2,1,0:T(8,128)} copy(f32[20,4,16,1024]{3,1,2,0:T(4,128)} %bitcast.94) | data formatting | bytes 10485760 | tf_op jit(solution)/shard_map/all_to_all | solution.py:83
  644.6 4.6 reduce_sum.9
  651.9 9.0 %all_gather.3 = f32[5,32,1024]{2,1,0:T(8,128)S(1)} all-gather(f32[5,8,1024]{2,1,0:T(8,128)S(1)} %bitcast_multiply_fusion), channel_id=1, replica_groups=mesh['az'=4,'rad'=2,'ax'=4] {'ax'}, dimensions={1}, use_global_device_ids=true | all-gather | bytes 819200 | tf_op jit(solution)/shard_map/all_gather | solution.py:88
  708.6 5.5 multiply_add_fusion.2
  (75 shorter events, 62.1 us)
Async XLA Ops:
  8.8 144.1 %all-to-all-start = ((f32[20,64,1024]{2,0,1:T(8,128)}), f32[20,64,1024]{2,0,1:T(8,128)}, u32[]{:S(2)}, u32[]{:S(2)}) async-start(f32[20,64,1024]{2,0,1:T(8,128)} %copy.187), calls=%async_computation | async-start | bytes 12582912 | tf_op jit(solution)/shard_map/all_to_all | solution.py:81
  182.9 8.7 %copy-start.2 = (f32[320,64,64]{0,1,2:T(8,128)S(1)}, f32[320,64,64]{0,1,2:T(8,128)}, u32[]{:S(2)}) copy-start(f32[320,64,64]{0,1,2:T(8,128)} %copy.191) | copy-start | bytes 15728644
  199.2 27.2 %copy-start.1 = (f32[320,64,64]{0,1,2:T(8,128)}, f32[320,64,64]{0,1,2:T(8,128)S(1)}, u32[]{:S(2)}) copy-start(f32[320,64,64]{0,1,2:T(8,128)S(1)} %get-tuple-element.17) | copy-start | bytes 15728644
  258.9 10.3 %copy-start = (f32[320,64,64]{0,2,1:T(8,128)S(1)}, f32[320,64,64]{0,2,1:T(8,128)}, u32[]{:S(2)}) copy-start(f32[320,64,64]{0,2,1:T(8,128)} %get-tuple-element.14) | copy-start | bytes 15728644
  300.1 12.4 %copy-start.3 = (f32[320,64,64]{0,2,1:T(8,128)S(1)}, f32[320,64,64]{0,2,1:T(8,128)}, u32[]{:S(2)}) copy-start(f32[320,64,64]{0,2,1:T(8,128)} %get-tuple-element.12) | copy-start | bytes 15728644
  420.9 5.2 copy-start.4
  420.9 120.3 %all-to-all-start.1 = ((f32[4,1,327680]{2,1,0:T(1,128)}), f32[4,1,327680]{2,1,0:T(1,128)}, u32[]{:S(2)}, u32[]{:S(2)}) async-start(f32[4,1,327680]{2,1,0:T(1,128)} %reshape.131), calls=%async_computation.1 | async-start | bytes 10485760 | tf_op jit(solution)/shard_map/all_to_all | solution.py:83
  426.5 12.6 %copy-start.6 = (s32[32,2]{0,1:T(2,128)S(1)}, s32[32,2]{0,1:T(2,128)}, u32[]{:S(2)}) copy-start(s32[32,2]{0,1:T(2,128)} %param.9) | copy-start | bytes 772
  427.5 233.4 %collective-permute-start.3 = (f32[5,32,1,1024]{3,1,0,2:T(8,128)}, f32[5,32,1,1024]{3,1,0,2:T(8,128)}, u32[]{:S(2)}, u32[]{:S(2)}) collective-permute-start(f32[5,32,1,1024]{3,1,0,2:T(8,128)} %get-tuple-element.30), channel_id=1, source_target_pairs={{0,1},{1,2},{2,3},{4,5},{5,6},{6,7},{8,9},{9,10},{10,11},{12,13},{... | collective-permute-start | bytes 1966088 | tf_op jit(solution)/shard_map/ppermute | solution.py:21
  431.8 230.3 %collective-permute-start.2 = (f32[5,32,1,1024]{3,1,0,2:T(8,128)S(1)}, f32[5,32,1,1024]{3,1,0,2:T(8,128)}, u32[]{:S(2)}, u32[]{:S(2)}) collective-permute-start(f32[5,32,1,1024]{3,1,0,2:T(8,128)S(1)} %get-tuple-element.31), channel_id=1, source_target_pairs={{1,0},{2,1},{3,2},{5,4},{6,5},{7,6},{9,8},{10,9},{11,10},{13,12},{... | collective-permute-start | bytes 1966088 | tf_op jit(solution)/shard_map/ppermute | solution.py:22
  433.8 228.3 %collective-permute-start = (f32[5,1,2,1024]{3,1,0,2:T(1,128)S(1)}, f32[5,1,2,1024]{3,1,0,2:T(1,128)S(1)}, u32[]{:S(2)}, u32[]{:S(2)}) collective-permute-start(f32[5,1,2,1024]{3,1,0,2:T(1,128)S(1)} %copy.181), channel_id=1, source_target_pairs={{4,0},{5,1},{6,2},{7,3},{12,8},{13,9},{14,10},{15,11},{20,16},{21,... | collective-permute-start | bytes 122888 | tf_op jit(solution)/shard_map/ppermute | solution.py:22
  435.1 227.0 %collective-permute-start.1 = (f32[5,1,2,1024]{3,1,0,2:T(1,128)S(1)}, f32[5,1,2,1024]{3,1,0,2:T(1,128)S(1)}, u32[]{:S(2)}, u32[]{:S(2)}) collective-permute-start(f32[5,1,2,1024]{3,1,0,2:T(1,128)S(1)} %copy.183), channel_id=1, source_target_pairs={{0,4},{1,5},{2,6},{3,7},{8,12},{9,13},{10,14},{11,15},{16,20},{17,... | collective-permute-start | bytes 122888 | tf_op jit(solution)/shard_map/ppermute | solution.py:21
  644.6 4.6 copy-start.7
  651.9 10.2 %copy-start.5 = (f32[5]{0:T(128)S(1)}, f32[5]{0:T(128)}, u32[]{:S(2)}) copy-start(f32[5]{0:T(128)} %constant.78) | copy-start | bytes 64
  664.2 9.9 %collective-permute-start.7 = (f32[5,32,1,1024]{3,1,0,2:T(8,128)S(1)}, f32[5,32,1,1024]{3,1,0,2:T(8,128)S(1)}, u32[]{:S(2)}, u32[]{:S(2)}) collective-permute-start(f32[5,32,1,1024]{3,1,0,2:T(8,128)S(1)} %get-tuple-element.28), channel_id=1, source_target_pairs={{0,1},{1,2},{2,3},{4,5},{5,6},{6,7},{8,9},{9,10},{10,11},{12,13},{... | collective-permute-start | bytes 1966088 | tf_op jit(solution)/shard_map/ppermute | solution.py:21
  666.7 11.9 %collective-permute-start.6 = (f32[5,32,1,1024]{3,1,0,2:T(8,128)S(1)}, f32[5,32,1,1024]{3,1,0,2:T(8,128)S(1)}, u32[]{:S(2)}, u32[]{:S(2)}) collective-permute-start(f32[5,32,1,1024]{3,1,0,2:T(8,128)S(1)} %get-tuple-element.29), channel_id=1, source_target_pairs={{1,0},{2,1},{3,2},{5,4},{6,5},{7,6},{9,8},{10,9},{11,10},{13,12},{... | collective-permute-start | bytes 1966088 | tf_op jit(solution)/shard_map/ppermute | solution.py:22
  668.7 5.6 collective-permute-start.4
  670.0 5.2 collective-permute-start.5
  679.8 10.0 %collective-permute-start.11 = (f32[5,32,1,1024]{3,1,0,2:T(8,128)S(1)}, f32[5,32,1,1024]{3,1,0,2:T(8,128)S(1)}, u32[]{:S(2)}, u32[]{:S(2)}) collective-permute-start(f32[5,32,1,1024]{3,1,0,2:T(8,128)S(1)} %get-tuple-element.24), channel_id=1, source_target_pairs={{0,1},{1,2},{2,3},{4,5},{5,6},{6,7},{8,9},{9,10},{10,11},{12,13},{... | collective-permute-start | bytes 1966088 | tf_op jit(solution)/shard_map/ppermute | solution.py:21
  681.7 11.9 %collective-permute-start.10 = (f32[5,32,1,1024]{3,1,0,2:T(8,128)S(1)}, f32[5,32,1,1024]{3,1,0,2:T(8,128)S(1)}, u32[]{:S(2)}, u32[]{:S(2)}) collective-permute-start(f32[5,32,1,1024]{3,1,0,2:T(8,128)S(1)} %get-tuple-element.25), channel_id=1, source_target_pairs={{1,0},{2,1},{3,2},{5,4},{6,5},{7,6},{9,8},{10,9},{11,10},{13,12},{... | collective-permute-start | bytes 1966088 | tf_op jit(solution)/shard_map/ppermute | solution.py:22
  684.2 5.7 collective-permute-start.8
  685.5 5.2 collective-permute-start.9
  694.8 9.7 %collective-permute-start.15 = (f32[5,32,1,1024]{3,1,0,2:T(8,128)S(1)}, f32[5,32,1,1024]{3,1,0,2:T(8,128)S(1)}, u32[]{:S(2)}, u32[]{:S(2)}) collective-permute-start(f32[5,32,1,1024]{3,1,0,2:T(8,128)S(1)} %get-tuple-element.20), channel_id=1, source_target_pairs={{0,1},{1,2},{2,3},{4,5},{5,6},{6,7},{8,9},{9,10},{10,11},{12,13},{... | collective-permute-start | bytes 1966088 | tf_op jit(solution)/shard_map/ppermute | solution.py:21
  696.7 11.9 %collective-permute-start.14 = (f32[5,32,1,1024]{3,1,0,2:T(8,128)S(1)}, f32[5,32,1,1024]{3,1,0,2:T(8,128)S(1)}, u32[]{:S(2)}, u32[]{:S(2)}) collective-permute-start(f32[5,32,1,1024]{3,1,0,2:T(8,128)S(1)} %get-tuple-element.21), channel_id=1, source_target_pairs={{1,0},{2,1},{3,2},{5,4},{6,5},{7,6},{9,8},{10,9},{11,10},{13,12},{... | collective-permute-start | bytes 1966088 | tf_op jit(solution)/shard_map/ppermute | solution.py:22
  699.2 5.4 collective-permute-start.12
  700.5 5.2 collective-permute-start.13
where the time goes:
time: 722 us; the launch traced here: 716 us
  waiting for transfers between devices  252 us (35%)
  local copies, waits for them, and re-layouts  225 us (31%)
  matrix products  143 us (20%)
  starting transfers between devices  51.5 us (7%)
  other arithmetic  34.3 us (5%)
  blocking collectives  8.99 us (1%)
    all_to_all x1, waiting for transfers between devices, on_device(): lax.all_to_all(stacked, 'az', split_axis=1, concat_axis=2, tiled=True)  137 us
    unnamed x20, local copies, waits for them, and re-layouts  112 us
    all_to_all x1, waiting for transfers between devices, on_device(): lax.all_to_all(moved, 'az', split_axis=2, concat_axis=1, tiled=True)  102 us
    all_to_all x3, local copies, waits for them, and re-layouts, on_device(): lax.all_to_all(moved, 'az', split_axis=2, concat_axis=1, tiled=True)  32.1 us
    another operation x2, local copies, waits for them, and re-layouts, on_device(): spectral_shift(piece.reshape(-1, piece.shape[2]), shift_value)  28.5 us
    ppermute x8, starting transfers between devices, padded(): before = lax.ppermute(last, axis, up)  26.7 us
    another operation x2, local copies, waits for them, and re-layouts, spectral_shift(): grid = rows.reshape(count, outer, inner)  21.5 us
    dot_general x1, matrix products, spectral_shift(): jnp.einsum('bkq,qm->bkm', twist_im, cos_inner, precision=hp)  19.1 us
  transfers between devices with their start and end apart: 18, of which 9 were waited for; matrix products, arithmetic and copies ran while one was open for 16% of the time, Pallas kernels for 0%

commit v1 on v0

--- a/solution.py
+++ b/solution.py
@@ -80,7 +80,10 @@
     shift_value = shift[0]
     piece = lax.all_to_all(stacked, "az", split_axis=1, concat_axis=2, tiled=True)
     moved = spectral_shift(piece.reshape(-1, piece.shape[2]), shift_value).reshape(piece.shape)
-    shifted_flat = lax.all_to_all(moved, "az", split_axis=2, concat_axis=1, tiled=True)
+    size = lax.axis_size("az")
+    blocks = jnp.stack(jnp.split(moved, size, axis=2), axis=0)
+    blocks = lax.all_to_all(blocks, "az", split_axis=0, concat_axis=0)
+    shifted_flat = jnp.concatenate(blocks, axis=1)
     shifted_cycle = shifted_flat.reshape(layers, variables, radial, sector)
     weights = jnp.array(LAYER_WEIGHTS, jnp.float32)
     depth, count, rows, width = shifted_cycle.shape

time: 722 us -> 556 us (0.77)
  local copies, waits for them, and re-layouts: 225 us -> 73.6 us
  other arithmetic: 34.3 us -> 19 us
    unnamed x20 -> x18, local copies, waits for them, and re-layouts: 112 us -> 2.53 us
    all_to_all x3 -> x0, local copies, waits for them, and re-layouts: 32.1 us -> none  [on_device(): lax.all_to_all(moved, 'az', split_axis=2, concat_axis=1, tiled=True)]
    another operation x2 -> x1, local copies, waits for them, and re-layouts: 28.5 us -> 9.73 us  [on_device(): spectral_shift(piece.reshape(-1, piece.shape[2]), shift_value)]
    all_to_all x1 -> x0, other arithmetic: 18.3 us -> none  [on_device(): lax.all_to_all(moved, 'az', split_axis=2, concat_axis=1, tiled=True)]
  transfers between devices with their start and end apart: 18 -> 18, of which waited for: 9 -> 10; matrix products, arithmetic and copies ran while one was open for 16% -> 3% of each run, Pallas kernels for 0% -> 0%
where the time goes in v1:
time: 556 us; the launch traced here: 551 us
  waiting for transfers between devices  254 us (46%)
  matrix products  143 us (26%)
  local copies, waits for them, and re-layouts  73.6 us (13%)
  starting transfers between devices  50.4 us (9%)
  other arithmetic  19 us (3%)
  blocking collectives  9.05 us (2%)
    all_to_all x1, waiting for transfers between devices, on_device(): lax.all_to_all(stacked, 'az', split_axis=1, concat_axis=2, tiled=True)  137 us
    all_to_all x1, waiting for transfers between devices, on_device(): blocks = lax.all_to_all(blocks, 'az', split_axis=0, concat_axis=0)  101 us
    ppermute x8, starting transfers between devices, padded(): before = lax.ppermute(last, axis, up)  24.1 us
    another operation x2, local copies, waits for them, and re-layouts, spectral_shift(): grid = rows.reshape(count, outer, inner)  21.4 us
    dot_general x1, matrix products, spectral_shift(): jnp.einsum('bkq,qm->bkm', twist_im, cos_inner, precision=hp)  19.1 us
    ppermute x8, starting transfers between devices, padded(): after = lax.ppermute(leading, axis, down)  15.2 us
    dot_general x1, matrix products, spectral_shift(): jnp.einsum('bkm,qm->bkq', mixed_im, cos_inner, precision=hp)  15 us
    dot_general x1, matrix products, spectral_shift(): jnp.einsum('bkq,qm->bkm', twist_re, sin_inner, precision=hp)  13.8 us
  transfers between devices with their start and end apart: 18, of which 10 were waited for; matrix products, arithmetic and copies ran while one was open for 3% of the time, Pallas kernels for 0%

profile of v1, /device:TPU:1, one launch (start us, length us, event | category | flops | bytes accessed | tf_op | source)
XLA Modules:
  0.0 551.3 jit_solution(4089097650420636597)
XLA Ops:
  0.6 8.2 %copy.151 = f32[20,64,1024]{2,0,1:T(8,128)} copy(f32[20,64,1024]{2,1,0:T(8,128)} %bitcast.99) | data formatting | bytes 10485760 | tf_op jit(solution)/shard_map/reshape | solution.py:79
  8.8 6.0 %all-to-all-start = ((f32[20,64,1024]{2,0,1:T(8,128)}), f32[20,64,1024]{2,0,1:T(8,128)}, u32[]{:S(2)}, u32[]{:S(2)}) async-start(f32[20,64,1024]{2,0,1:T(8,128)} %copy.151), calls=%async_computation | async-start | bytes 12582912 | tf_op jit(solution)/shard_map/all_to_all | solution.py:81
  15.9 137.3 %all-to-all-done = f32[20,64,1024]{2,0,1:T(8,128)} async-done(((f32[20,64,1024]{2,0,1:T(8,128)}), f32[20,64,1024]{2,0,1:T(8,128)}, u32[]{:S(2)}, u32[]{:S(2)}) %all-to-all-start) | async-done | bytes 5242912 | tf_op jit(solution)/shard_map/all_to_all | solution.py:81
  153.3 8.5 %copy.153 = f32[20,16,4,1024]{3,2,1,0:T(4,128)} copy(f32[20,16,4,1024]{3,0,1,2:T(8,128)} %bitcast.5) | data formatting | bytes 10485760 | tf_op jit(solution)/shard_map/all_to_all | solution.py:81
  161.8 9.6 %reshape_reshape.9 = f32[320,64,64]{2,1,0:T(8,128)} reshape(f32[20,16,4,1024]{3,2,1,0:T(4,128)} %copy.153) | data formatting | bytes 10485760 | tf_op jit(solution)/shard_map/reshape;reshape | solution.py:44
  171.4 11.8 %copy.155 = f32[320,64,64]{0,1,2:T(8,128)} copy(f32[320,64,64]{2,1,0:T(8,128)} %reshape_reshape.9) | data formatting | bytes 10485760 | tf_op jit(solution)/shard_map/reshape;reshape | solution.py:44
  183.2 8.7 %fusion.44 = f32[64,320,64]{1,0,2:T(8,128)S(1)} fusion(f32[320,64,64]{0,1,2:T(8,128)} %copy.155), kind=kOutput, calls=%fused_computation.90 | convolution fusion | flops 1006690304 | bytes 10485760 | tf_op jit(solution)/shard_map/bpq,pk->bkq/dot_general | solution.py:46
  191.9 7.6 %add_bitcast_fusion = (f32[320,64,64]{0,1,2:T(8,128)S(1)}, f32[320,64,64]{0,1,2:T(8,128)S(1)}) fusion(f32[64,320,64]{1,0,2:T(8,128)S(1)} %fusion.44, f32[64,64]{0,1:T(8,128)S(1)} %copy.159, f32[64,64]{0,1:T(8,128)S(1)} %copy.156, f32[320,64,64]{0,1,2:T(8,128)S(1)} %copy-done.2), kind=kOutput, calls=%fused_computation.10 | convolution fusion | flops 1015865344 | bytes 21004288 | tf_op jit(solution)/shard_map/bpq,pk->bkq/dot_general | solution.py:45
  199.5 13.8 %fusion.8 = f32[320,64,64]{0,2,1:T(8,128)} fusion(f32[320,64,64]{0,1,2:T(8,128)S(1)} %get-tuple-element.14), kind=kOutput, calls=%fused_computation.15 | convolution fusion | flops 1006690304 | bytes 10485760 | tf_op jit(solution)/shard_map/bkq,qm->bkm/dot_general | solution.py:52
  213.3 13.2 %fusion.10 = f32[320,64,64]{0,2,1:T(8,128)} fusion(f32[320,64,64]{0,1,2:T(8,128)S(1)} %get-tuple-element.14), kind=kOutput, calls=%fused_computation.17 | convolution fusion | flops 1006690304 | bytes 10485760 | tf_op jit(solution)/shard_map/bkq,qm->bkm/dot_general | solution.py:49
  226.5 13.6 %fusion.6 = f32[320,64,64]{0,2,1:T(8,128)} fusion(f32[320,64,64]{0,1,2:T(8,128)S(1)} %get-tuple-element.15), kind=kOutput, calls=%fused_computation.13 | convolution fusion | flops 1006690304 | bytes 10485760 | tf_op jit(solution)/shard_map/bkq,qm->bkm/dot_general | solution.py:49
  240.1 19.1 %multiply_subtract_fusion.1 = (f32[320,64,64]{0,2,1:T(8,128)}, f32[320,64,64]{0,2,1:T(8,128)S(1)}) fusion(f32[64,64]{1,0:T(8,128)S(1)} %get-tuple-element.37, f32[64,64]{1,0:T(8,128)S(1)} %get-tuple-element.36, f32[320,64,64]{0,2,1:T(8,128)} %fusion.8, f32[320,64,64]{0,2,1:T(8,128)} %fusion.10, f32[320,64,64]{0,2,1:T(8,128)} %fusion.6, ...), kind=kOutput, calls=%fused_computation.8 | convolution fusion | flops 1017176064 | bytes 31490048 | tf_op jit(solution)/shard_map/bkq,qm->bkm/dot_general | solution.py:52
  259.2 10.2 %fusion.38 = f32[320,64,64]{0,2,1:T(8,128)} fusion(f32[320,64,64]{0,2,1:T(8,128)} %get-tuple-element.12), kind=kOutput, calls=%fused_computation.84 | convolution fusion | flops 1006690304 | bytes 10485760 | tf_op jit(solution)/shard_map/bkm,qm->bkq/dot_general | solution.py:66
  269.4 7.8 %fusion.53 = f32[320,64,64]{0,2,1:T(8,128)} fusion(f32[320,64,64]{0,2,1:T(8,128)S(1)} %copy-done), kind=kOutput, calls=%fused_computation.99 | convolution fusion | flops 1006690304 | bytes 10485760 | tf_op jit(solution)/shard_map/bkm,qm->bkq/dot_general | solution.py:63
  277.3 7.9 %fusion.40 = f32[320,64,64]{0,2,1:T(8,128)} fusion(f32[320,64,64]{0,2,1:T(8,128)S(1)} %get-tuple-element.13), kind=kOutput, calls=%fused_computation.86 | convolution fusion | flops 1006690304 | bytes 10485760 | tf_op jit(solution)/shard_map/bkm,qm->bkq/dot_general | solution.py:63
  285.2 15.0 %multiply_subtract_fusion = (f32[320,64,64]{0,2,1:T(8,128)}, f32[320,64,64]{0,2,1:T(8,128)}) fusion(f32[64,64]{1,0:T(8,128)S(1)} %get-tuple-element.38, f32[64,64]{1,0:T(8,128)S(1)} %get-tuple-element.39, f32[320,64,64]{0,2,1:T(8,128)} %fusion.38, f32[320,64,64]{0,2,1:T(8,128)} %fusion.53, f32[320,64,64]{0,2,1:T(8,128)} %fusion.40, ...), kind=kOutput, calls=%fused_computation.6 | convolution fusion | flops 1017176064 | bytes 31490048 | tf_op jit(solution)/shard_map/bkm,qm->bkq/dot_general | solution.py:66
  300.1 12.4 %fusion = f32[64,320,64]{1,0,2:T(8,128)S(1)} fusion(f32[320,64,64]{0,2,1:T(8,128)} %get-tuple-element.11), kind=kOutput, calls=%fused_computation | convolution fusion | flops 1006690304 | bytes 10485760 | tf_op jit(solution)/shard_map/bkq,pk->bpq/dot_general | solution.py:71
  312.5 11.4 %multiply_bitcast_fusion = f32[320,64,64]{0,1,2:T(8,128)} fusion(f32[64,320,64]{1,0,2:T(8,128)S(1)} %fusion, f32[320,64,64]{0,2,1:T(8,128)S(1)} %copy-done.3), kind=kOutput, calls=%fused_computation.4 | convolution fusion | flops 1009311744 | bytes 15728640 | tf_op jit(solution)/shard_map/bkq,pk->bpq/dot_general | solution.py:71
  324.0 12.5 %copy.170 = f32[320,64,64]{2,1,0:T(8,128)} copy(f32[320,64,64]{0,1,2:T(8,128)} %multiply_bitcast_fusion) | data formatting | bytes 10485760 | tf_op jit(solution)/shard_map/div | solution.py:74
  336.5 9.7 %reshape_reshape.10 = f32[20,16,4096]{2,1,0:T(8,128)} reshape(f32[320,64,64]{2,1,0:T(8,128)} %copy.170) | data formatting | bytes 10485760 | tf_op jit(solution)/shard_map/reshape;reshape | solution.py:82
  346.3 3.1 slice_bitcast_fusion.3
  352.5 5.2 all-to-all-start.1
  359.1 4.0 collective-permute-start.1
  364.5 3.7 collective-permute-start.2
  368.2 3.3 collective-permute-start.3
  371.5 101.3 %all-to-all-done.1 = f32[4,20,16,1024]{3,2,1,0:T(8,128)} async-done(((f32[4,20,16,1024]{3,2,1,0:T(8,128)}), f32[4,20,16,1024]{3,2,1,0:T(8,128)}, u32[]{:S(2)}, u32[]{:S(2)}) %all-to-all-start.1) | async-done | bytes 5242912 | tf_op jit(solution)/shard_map/all_to_all | solution.py:85
  472.8 5.7 %copy.171 = f32[20,4,16,1024]{3,2,1,0:T(8,128)} copy(f32[20,4,16,1024]{3,2,0,1:T(8,128)} %bitcast.20) | data formatting | bytes 10485760 | tf_op jit(solution)/shard_map/reshape | solution.py:86
  478.5 4.6 reduce_sum.9
  485.9 9.0 %all_gather.3 = f32[5,32,1024]{2,1,0:T(8,128)S(1)} all-gather(f32[5,8,1024]{2,1,0:T(8,128)S(1)} %bitcast_multiply_fusion), channel_id=1, replica_groups=mesh['az'=4,'rad'=2,'ax'=4] {'ax'}, dimensions={1}, use_global_device_ids=true | all-gather | bytes 819200 | tf_op jit(solution)/shard_map/all_gather | solution.py:91
  502.7 3.1 collective-permute-start.5
  535.5 4.0 collective-permute-start.13
  543.5 5.5 multiply_add_fusion.2
  (71 shorter events, 52.4 us)
Async XLA Ops:
  8.8 144.4 %all-to-all-start = ((f32[20,64,1024]{2,0,1:T(8,128)}), f32[20,64,1024]{2,0,1:T(8,128)}, u32[]{:S(2)}, u32[]{:S(2)}) async-start(f32[20,64,1024]{2,0,1:T(8,128)} %copy.151), calls=%async_computation | async-start | bytes 12582912 | tf_op jit(solution)/shard_map/all_to_all | solution.py:81
  183.2 8.7 %copy-start.2 = (f32[320,64,64]{0,1,2:T(8,128)S(1)}, f32[320,64,64]{0,1,2:T(8,128)}, u32[]{:S(2)}) copy-start(f32[320,64,64]{0,1,2:T(8,128)} %copy.155) | copy-start | bytes 15728644
  199.5 27.0 %copy-start.1 = (f32[320,64,64]{0,1,2:T(8,128)}, f32[320,64,64]{0,1,2:T(8,128)S(1)}, u32[]{:S(2)}) copy-start(f32[320,64,64]{0,1,2:T(8,128)S(1)} %get-tuple-element.15) | copy-start | bytes 15728644
  259.2 10.2 %copy-start = (f32[320,64,64]{0,2,1:T(8,128)S(1)}, f32[320,64,64]{0,2,1:T(8,128)}, u32[]{:S(2)}) copy-start(f32[320,64,64]{0,2,1:T(8,128)} %get-tuple-element.12) | copy-start | bytes 15728644
  300.1 12.4 %copy-start.3 = (f32[320,64,64]{0,2,1:T(8,128)S(1)}, f32[320,64,64]{0,2,1:T(8,128)}, u32[]{:S(2)}) copy-start(f32[320,64,64]{0,2,1:T(8,128)} %get-tuple-element.10) | copy-start | bytes 15728644
  352.5 5.2 copy-start.4
  352.5 120.4 %all-to-all-start.1 = ((f32[4,20,16,1024]{3,2,1,0:T(8,128)}), f32[4,20,16,1024]{3,2,1,0:T(8,128)}, u32[]{:S(2)}, u32[]{:S(2)}) async-start(f32[4,20,16,1024]{3,2,1,0:T(8,128)} %pad_maximum_fusion), calls=%async_computation.1 | async-start | bytes 10485760 | tf_op jit(solution)/shard_map/all_to_all | solution.py:85
  357.7 138.4 %collective-permute-start = (f32[5,1,2,1024]{3,1,0,2:T(1,128)S(1)}, f32[5,1,2,1024]{3,1,0,2:T(1,128)S(1)}, u32[]{:S(2)}, u32[]{:S(2)}) collective-permute-start(f32[5,1,2,1024]{3,1,0,2:T(1,128)S(1)} %copy.145), channel_id=1, source_target_pairs={{4,0},{5,1},{6,2},{7,3},{12,8},{13,9},{14,10},{15,11},{20,16},{21,... | collective-permute-start | bytes 122888 | tf_op jit(solution)/shard_map/ppermute | solution.py:22
  359.1 137.0 %collective-permute-start.1 = (f32[5,1,2,1024]{3,1,0,2:T(1,128)S(1)}, f32[5,1,2,1024]{3,1,0,2:T(1,128)S(1)}, u32[]{:S(2)}, u32[]{:S(2)}) collective-permute-start(f32[5,1,2,1024]{3,1,0,2:T(1,128)S(1)} %copy.147), channel_id=1, source_target_pairs={{0,4},{1,5},{2,6},{3,7},{8,12},{9,13},{10,14},{11,15},{16,20},{17,... | collective-permute-start | bytes 122888 | tf_op jit(solution)/shard_map/ppermute | solution.py:21
  363.5 8.0 %copy-start.6 = (s32[32,2]{0,1:T(2,128)S(1)}, s32[32,2]{0,1:T(2,128)}, u32[]{:S(2)}) copy-start(s32[32,2]{0,1:T(2,128)} %param.9) | copy-start | bytes 772
  364.5 131.6 %collective-permute-start.2 = (f32[5,32,1,1024]{3,1,0,2:T(8,128)S(1)}, f32[5,32,1,1024]{3,1,0,2:T(8,128)}, u32[]{:S(2)}, u32[]{:S(2)}) collective-permute-start(f32[5,32,1,1024]{3,1,0,2:T(8,128)S(1)} %get-tuple-element.33), channel_id=1, source_target_pairs={{1,0},{2,1},{3,2},{5,4},{6,5},{7,6},{9,8},{10,9},{11,10},{13,12},{... | collective-permute-start | bytes 1966088 | tf_op jit(solution)/shard_map/ppermute | solution.py:22
  368.2 126.7 %collective-permute-start.3 = (f32[5,32,1,1024]{3,1,0,2:T(8,128)}, f32[5,32,1,1024]{3,1,0,2:T(8,128)}, u32[]{:S(2)}, u32[]{:S(2)}) collective-permute-start(f32[5,32,1,1024]{3,1,0,2:T(8,128)} %get-tuple-element.32), channel_id=1, source_target_pairs={{0,1},{1,2},{2,3},{4,5},{5,6},{6,7},{8,9},{9,10},{10,11},{12,13},{... | collective-permute-start | bytes 1966088 | tf_op jit(solution)/shard_map/ppermute | solution.py:21
  478.5 4.6 copy-start.7
  485.8 10.3 %copy-start.5 = (f32[5]{0:T(128)S(1)}, f32[5]{0:T(128)}, u32[]{:S(2)}) copy-start(f32[5]{0:T(128)} %constant.78) | copy-start | bytes 64
  498.3 9.9 %collective-permute-start.7 = (f32[5,32,1,1024]{3,1,0,2:T(8,128)S(1)}, f32[5,32,1,1024]{3,1,0,2:T(8,128)S(1)}, u32[]{:S(2)}, u32[]{:S(2)}) collective-permute-start(f32[5,32,1,1024]{3,1,0,2:T(8,128)S(1)} %get-tuple-element.30), channel_id=1, source_target_pairs={{0,1},{1,2},{2,3},{4,5},{5,6},{6,7},{8,9},{9,10},{10,11},{12,13},{... | collective-permute-start | bytes 1966088 | tf_op jit(solution)/shard_map/ppermute | solution.py:21
  500.6 11.9 %collective-permute-start.6 = (f32[5,32,1,1024]{3,1,0,2:T(8,128)S(1)}, f32[5,32,1,1024]{3,1,0,2:T(8,128)S(1)}, u32[]{:S(2)}, u32[]{:S(2)}) collective-permute-start(f32[5,32,1,1024]{3,1,0,2:T(8,128)S(1)} %get-tuple-element.31), channel_id=1, source_target_pairs={{1,0},{2,1},{3,2},{5,4},{6,5},{7,6},{9,8},{10,9},{11,10},{13,12},{... | collective-permute-start | bytes 1966088 | tf_op jit(solution)/shard_map/ppermute | solution.py:22
  502.7 5.5 %collective-permute-start.5 = (f32[5,1,2,1024]{3,1,0,2:T(1,128)S(1)}, f32[5,1,2,1024]{3,1,0,2:T(1,128)S(1)}, u32[]{:S(2)}, u32[]{:S(2)}) collective-permute-start(f32[5,1,2,1024]{3,1,0,2:T(1,128)S(1)} %get-tuple-element.29), channel_id=1, source_target_pairs={{0,4},{1,5},{2,6},{3,7},{8,12},{9,13},{10,14},{11,15},{16,20},{17,... | collective-permute-start | bytes 122888 | tf_op jit(solution)/shard_map/ppermute | solution.py:21
  505.8 5.4 collective-permute-start.4
  513.7 10.4 %collective-permute-start.11 = (f32[5,32,1,1024]{3,1,0,2:T(8,128)S(1)}, f32[5,32,1,1024]{3,1,0,2:T(8,128)S(1)}, u32[]{:S(2)}, u32[]{:S(2)}) collective-permute-start(f32[5,32,1,1024]{3,1,0,2:T(8,128)S(1)} %get-tuple-element.26), channel_id=1, source_target_pairs={{0,1},{1,2},{2,3},{4,5},{5,6},{6,7},{8,9},{9,10},{10,11},{12,13},{... | collective-permute-start | bytes 1966088 | tf_op jit(solution)/shard_map/ppermute | solution.py:21
  516.6 11.9 %collective-permute-start.10 = (f32[5,32,1,1024]{3,1,0,2:T(8,128)S(1)}, f32[5,32,1,1024]{3,1,0,2:T(8,128)S(1)}, u32[]{:S(2)}, u32[]{:S(2)}) collective-permute-start(f32[5,32,1,1024]{3,1,0,2:T(8,128)S(1)} %get-tuple-element.27), channel_id=1, source_target_pairs={{1,0},{2,1},{3,2},{5,4},{6,5},{7,6},{9,8},{10,9},{11,10},{13,12},{... | collective-permute-start | bytes 1966088 | tf_op jit(solution)/shard_map/ppermute | solution.py:22
  518.6 5.6 %collective-permute-start.9 = (f32[5,1,2,1024]{3,1,0,2:T(1,128)S(1)}, f32[5,1,2,1024]{3,1,0,2:T(1,128)S(1)}, u32[]{:S(2)}, u32[]{:S(2)}) collective-permute-start(f32[5,1,2,1024]{3,1,0,2:T(1,128)S(1)} %get-tuple-element.25), channel_id=1, source_target_pairs={{0,4},{1,5},{2,6},{3,7},{8,12},{9,13},{10,14},{11,15},{16,20},{17,... | collective-permute-start | bytes 122888 | tf_op jit(solution)/shard_map/ppermute | solution.py:21
  521.1 5.4 collective-permute-start.8
  529.7 9.7 %collective-permute-start.15 = (f32[5,32,1,1024]{3,1,0,2:T(8,128)S(1)}, f32[5,32,1,1024]{3,1,0,2:T(8,128)S(1)}, u32[]{:S(2)}, u32[]{:S(2)}) collective-permute-start(f32[5,32,1,1024]{3,1,0,2:T(8,128)S(1)} %get-tuple-element.22), channel_id=1, source_target_pairs={{0,1},{1,2},{2,3},{4,5},{5,6},{6,7},{8,9},{9,10},{10,11},{12,13},{... | collective-permute-start | bytes 1966088 | tf_op jit(solution)/shard_map/ppermute | solution.py:21
  531.6 11.9 %collective-permute-start.14 = (f32[5,32,1,1024]{3,1,0,2:T(8,128)S(1)}, f32[5,32,1,1024]{3,1,0,2:T(8,128)S(1)}, u32[]{:S(2)}, u32[]{:S(2)}) collective-permute-start(f32[5,32,1,1024]{3,1,0,2:T(8,128)S(1)} %get-tuple-element.23), channel_id=1, source_target_pairs={{1,0},{2,1},{3,2},{5,4},{6,5},{7,6},{9,8},{10,9},{11,10},{13,12},{... | collective-permute-start | bytes 1966088 | tf_op jit(solution)/shard_map/ppermute | solution.py:22
  534.2 5.4 collective-permute-start.12
  535.5 5.2 collective-permute-start.13
